TPU v7x, 512 devices: a whole 4x4x16 slice. The times are simulated.
512 devices in a mesh: chan: 16 (over y, x), patch: 32 (over z, core).
Axes of the slice: x: 4, y: 4, z: 16, core: 2. Of those that a mesh axis runs over, the one named last changes fastest.
Arguments:
- sky_maps: float32 [64, 393216], P('chan', 'patch')
- mode_vectors: float32 [64, 8], replicated
- pixel_weight: float32 [393216], P('patch'), may hold values from 0.3 to 3
- neighbours: int32 [48, 64, 9], P('chan', 'patch'), may hold values from 0 to 8, as said below
- tile_counts: int32 [48, 64], P('chan', 'patch'), may hold values from 0 to 9, as said below
- pair_bins: int32 [9, 128, 128], replicated, may hold values from 0 to 8, as said below
Outputs:
- correlation: float32 [16, 32, 8, 64, 64], P('chan', 'patch')
- covariance: float32 [64, 64], replicated
Inputs may be any that keep to these rules, and one draw needn't show every extreme that they name: `neighbours`: for tile (A, B) the first tile_counts[A, B] entries are distinct offset codes o in ascending order, each naming the tile (A + o // 3 - 1, B + o % 3 - 1), which lies inside the grid and is observed; later entries mean nothing. An observed tile lists code 4 (itself); if a tile lists another, that one lists it back. `tile_counts`: 0 exactly for tiles that are not observed; some tile has 9. `pair_bins`: one table for each offset code, the same for every tile pair with that offset; the value 8 marks a pair beyond the last bin.
All inputs are finite; a program needn't handle non-finite values.
Results may differ from a plain program's by a relative error of at most 0.00075.
Values may be sent and summed in bfloat16 or wider, within the bound.
A program may use at most 64 MiB of HBM per device.

v0:
```python
import math

import jax
import jax.numpy as jnp
from jax import lax
from jax.sharding import PartitionSpec as P

NCH = 64
MODES = 8
TILE = 128
NBIN = 8
NBR = 9
TA = 3
TB = 2


def padded(cells, sides, width):
    for axis, dim in sides:
        count = lax.axis_size(axis)
        ends = count - 1
        head = lax.slice_in_dim(cells, 0, width, axis=dim)
        tail = lax.slice_in_dim(cells, cells.shape[dim] - width, cells.shape[dim], axis=dim)
        cells = jnp.concatenate(
            [
                lax.ppermute(tail, axis, [(i, (i + 1) % count) for i in range(ends)]),
                cells,
                lax.ppermute(head, axis, [((i + 1) % count, i) for i in range(ends)]),
            ],
            axis=dim,
        )
    return cells


def orthonormal_basis(mode_vectors):
    columns = []
    for number in range(MODES):
        vector = mode_vectors[:, number]
        for earlier in columns:
            vector = vector - jnp.sum(earlier * vector) * earlier
        columns.append(vector / jnp.sqrt(jnp.sum(vector * vector) + 1e-06))
    return jnp.stack(columns, axis=1)


def projector(mode_vectors):
    basis = orthonormal_basis(mode_vectors)
    outer = jnp.dot(
        basis, basis.T, precision=lax.Precision.HIGHEST, preferred_element_type=jnp.float32
    )
    return jnp.eye(NCH, dtype=jnp.float32) - outer


def bin_masks(pair_bins):
    levels = jnp.arange(NBIN, dtype=jnp.int32)
    table = pair_bins[:, :, None, :] == levels[None, None, :, None]
    return table.astype(jnp.bfloat16).reshape(NBR, TILE, NBIN * TILE)


def taper_table():
    return 0.75 + 0.25 * jnp.cos(math.pi * jnp.arange(NBIN, dtype=jnp.float32) / NBIN)


def clean_block(project, gathered, weight_part):
    cleaned = jnp.dot(
        project, gathered, precision=lax.Precision.HIGHEST, preferred_element_type=jnp.float32
    )
    weighted = (cleaned * weight_part[None, :]).astype(jnp.bfloat16)
    return jnp.concatenate([weighted, weight_part.astype(jnp.bfloat16)[None, :]], axis=0)


def per_device(sky_maps, mode_vectors, pixel_weight, neighbours, tile_counts, pair_bins):
    chan_count = lax.axis_size("chan")
    chan_index = lax.axis_index("chan")
    local_channels = sky_maps.shape[0]
    project = projector(mode_vectors)
    block_pixels = TA * TB * TILE
    blocks = sky_maps.reshape(local_channels, chan_count, block_pixels)
    regrouped = lax.all_to_all(blocks, "chan", split_axis=1, concat_axis=0, tiled=True)
    gathered = regrouped.reshape(NCH, block_pixels)
    weight_part = lax.dynamic_slice_in_dim(pixel_weight, chan_index * block_pixels, block_pixels)
    own_tiles = clean_block(project, gathered, weight_part).reshape(NCH + 1, TA, TB, TILE)
    extended = padded(own_tiles, (("chan", 1), ("patch", 2)), 1)
    core_maps = own_tiles[:NCH]
    observed = tile_counts > 0
    masked = jnp.where(observed[None, :, :, None], core_maps, jnp.zeros((), jnp.bfloat16))
    partial_cov = jnp.einsum("cabq,dabq->cd", masked, core_maps, preferred_element_type=jnp.float32)
    pixel_total = jnp.sum(observed.astype(jnp.float32)) * TILE
    cov_sum, pixel_sum = lax.psum((partial_cov, pixel_total), ("chan", "patch"))
    covariance = cov_sum / pixel_sum
    mask_table = bin_masks(pair_bins)
    start_sums = jnp.zeros((NBIN, NCH + 1, NCH + 1), jnp.float32)
    centres = extended[:, 1 : TA + 1, 1 : TB + 1].reshape(NCH + 1, TA * TB, TILE)
    slot_live = jnp.arange(NBR, dtype=jnp.int32)[None, None, :] < tile_counts[:, :, None]
    pair_sums = start_sums
    for offset_code in range(NBR):
        row_shift = offset_code // 3
        col_shift = offset_code % 3
        partners = extended[:, row_shift : row_shift + TA, col_shift : col_shift + TB].reshape(
            NCH + 1, TA * TB, TILE
        )
        present = jnp.any((neighbours == offset_code) & slot_live, axis=-1)
        present = present.reshape(1, TA * TB, 1).astype(jnp.bfloat16)
        binned = jnp.einsum(
            "ctq,qk->ctk", centres, mask_table[offset_code], preferred_element_type=jnp.float32
        )
        binned = binned.astype(jnp.bfloat16) * present
        binned = binned.reshape(NCH + 1, TA * TB, NBIN, TILE)
        pair_sums = pair_sums + jnp.einsum(
            "ctbr,dtr->bcd", binned, partners, preferred_element_type=jnp.float32
        )
    spread = jnp.sqrt(jnp.diagonal(covariance) + 1e-06)
    norm_scale = spread[:, None] * spread[None, :]
    pair_weight = jnp.maximum(pair_sums[:, NCH, NCH], 1.0)
    correlation = taper_table()[:, None, None] * pair_sums[:, :NCH, :NCH]
    correlation = correlation / (pair_weight[:, None, None] * norm_scale[None])
    return (correlation[None, None], covariance)


def solution(mesh):
    return jax.shard_map(
        per_device,
        mesh=mesh,
        in_specs=(
            P("chan", "patch"),
            P(),
            P("patch"),
            P("chan", "patch", None),
            P("chan", "patch"),
            P(),
        ),
        out_specs=(P("chan", "patch", None, None, None), P()),
        check_vma=False,
    )
```

profile of v0, /device:TPU:1, one launch (start us, length us, event | category | flops | bytes accessed | tf_op | source)
XLA Modules:
  0.0 241.6 jit_solution(397972845415580127)
XLA Ops:
  0.6 7.6 %all-to-all-start = ((f32[4,16,768]{2,0,1:T(4,128)}), f32[4,16,768]{2,0,1:T(4,128)S(1)}, u32[]{:S(2)}, u32[]{:S(2)}) async-start(f32[4,16,768]{2,0,1:T(4,128)} %bitcast.252), calls=%async_computation | async-start | bytes 393216 | tf_op jit(solution)/shard_map/all_to_all | solution.py:77
  9.0 1.4 convert_reduce_fusion
  12.4 1.4 fusion.42
  13.8 2.3 fusion.36
  16.7 2.6 %multiply_reduce_fusion.26 = (f32[]{:T(128)}, f32[64]{0:T(128)S(1)}, f32[64]{0:T(128)S(1)}) fusion(f32[64,1]{0,1:T(1,128)S(1)} %get-tuple-element.82, f32[]{:T(128)} %get-tuple-element.17, f32[64,8]{0,1:T(8,128)} %param.7, f32[]{:T(128)S(6)} %sqrt.36, f32[]{:T(128)} %get-tuple-element.81), kind=kLoop, calls=%fused_computation.174 | loop fusion | flops 447 | bytes 1296 | tf_op jit(solution)/shard_map/reduce_sum | solution.py:39
  19.2 5.3 %multiply_reduce_fusion.6 = (f32[]{:T(128)}, f32[]{:T(128)}, f32[]{:T(128)}, f32[]{:T(128)}, f32[]{:T(128)}, /*index=5*/f32[]{:T(128)}, f32[64]{0:T(128)S(1)}, f...) fusion(f32[64]{0:T(128)S(1)} %get-tuple-element.80, f32[64]{0:T(128)S(1)} %get-tuple-element.79, ...), kind=kLoop, calls=%fused_computation.134 | loop fusion | flops 1530 | bytes 3376 | tf_op jit(solution)/shard_map/reduce_sum | solution.py:39
  25.2 4.4 %multiply_reduce_fusion.5 = (f32[]{:T(128)}, f32[]{:T(128)}, f32[]{:T(128)}, f32[]{:T(128)}, f32[]{:T(128)}, /*index=5*/f32[64]{0:T(128)S(1)}) fusion(f32[64]{0:T(128)S(1)} %get-tuple-element.77, f32[64]{0:T(128)S(1)} %get-tuple-element.80, f32[]{:T(128)} %get-tuple-element.36, f32[64]{0:T(128)S(1)} %get-tuple-element.76, f32[]{:T(128)} %get-tuple-element.37, ...), kind=kLoop, calls=%fused_computation.132 | loop fusion | flops 1467 | bytes 2096 | tf_op jit(solution)/shard_map/reduce_sum | solution.py:39
  29.6 1.9 multiply_reduce_fusion.22
  32.1 1.9 multiply_reduce_fusion.19
  34.0 5.1 %multiply_reduce_fusion.4 = (f32[]{:T(128)}, f32[]{:T(128)}, f32[]{:T(128)}, f32[]{:T(128)}, f32[64]{0:T(128)S(1)}, /*index=5*/f32[64]{0:T(128)S(1)}, f32[64]{0:T(128)S(1)}) fusion(f32[64]{0:T(128)S(1)} %get-tuple-element.69, f32[64]{0:T(128)S(1)} %get-tuple-element.68, f32[]{:T(128)} %get-tuple-element.67, f32[64]{0:T(128)S(1)} %get-tuple-element.72, ...), kind=kLoop, calls=%fused_computation.130 | loop fusion | flops 1404 | bytes 2604 | tf_op jit(solution)/shard_map/reduce_sum | solution.py:39
  39.7 3.2 %multiply_reduce_fusion.3 = (f32[]{:T(128)}, f32[]{:T(128)}, f32[]{:T(128)}, f32[64]{0:T(128)S(1)}) fusion(f32[64]{0:T(128)S(1)} %get-tuple-element.66, f32[64]{0:T(128)S(1)} %get-tuple-element.69, f32[]{:T(128)} %get-tuple-element.32, f32[64]{0:T(128)S(1)} %get-tuple-element.65, f32[]{:T(128)} %get-tuple-element.33, f32[64]{0:T(128)S(1)} %get-tuple-element.64, ...), kind=kLoop, calls=%fused_computation.128 | loop fusion | flops 957 | bytes 1568 | tf_op jit(solution)/shard_map/reduce_sum | solution.py:39
  42.9 2.0 multiply_reduce_fusion.13
  45.6 2.0 multiply_reduce_fusion.8
  47.5 2.4 multiply_reduce_fusion.2
  50.7 1.9 multiply_reduce_fusion.1
  52.6 1.9 multiply_reduce_fusion
  55.1 18.4 %subtract_divide_fusion = (f32[64,1]{0,1:T(1,128)S(1)}, f32[64,1]{0,1:T(1,128)S(1)}, f32[64,1]{0,1:T(1,128)S(1)}, f32[64,1]{0,1:T(1,128)S(1)}, f32[64,1]{0,1:T(1...) fusion(f32[64,1]{0,1:T(1,128)S(1)} %get-tuple-element.82, f32[]{:T(128)S(6)} %sqrt.42, f32[]{:T(128)} %get-tuple-element.55, ...), kind=kLoop, calls=%fused_computation.123 | loop fusion | flops 4032 | bytes 3980 | tf_op jit(solution)/shard_map/div | solution.py:40
  73.6 1.7 iota_compare_fusion
  81.2 3.3 %collective-permute-start = (bf16[65,1,2,128]{3,2,1,0:T(2,128)(2,1)S(1)}, bf16[65,1,2,128]{3,2,1,0:T(2,128)(2,1)S(1)}, u32[]{:S(2)}, u32[]{:S(2)}) collective-permute-start(bf16[65,1,2,128]{3,2,1,0:T(2,128)(2,1)S(1)} %get-tuple-element.102), channel_id=1, source_target_pairs={{0,32},{32,64},{64,96},{96,128},{128,160},{160,192},{192,224},{224... | collective-permute-start | bytes 99848 | tf_op jit(solution)/shard_map/ppermute | solution.py:25
  86.0 112.4 %all-reduce = (f32[64,64]{1,0:T(8,128)S(1)}, f32[]{:T(128)}) all-reduce(f32[64,64]{1,0:T(8,128)S(1)} %fusion.30, f32[]{:T(128)S(6)} %mul.782), channel_id=1, replica_groups=mesh['chan'=16,'patch'=32] {'chan','patch'}, use_global_device_ids=true, to_apply=%region_45.46 | all-reduce | flops 4097 | bytes 32776 | tf_op jit(solution)/shard_map/psum | solution.py:87
  200.7 1.3 fusion.1
  202.0 1.3 fusion.7
  203.4 1.4 fusion.5
  204.8 1.3 fusion.2
  207.4 1.3 fusion.4
  210.7 1.5 reshape.240
  213.3 3.3 %collective-permute-start.2 = (bf16[65,5,1,128]{3,2,1,0:T(2,128)(2,1)}, bf16[65,5,1,128]{3,2,1,0:T(2,128)(2,1)S(1)}, u32[]{:S(2)}, u32[]{:S(2)}) collective-permute-start(bf16[65,5,1,128]{3,2,1,0:T(2,128)(2,1)} %get-tuple-element.98), channel_id=1, source_target_pairs={{0,1},{1,2},{2,3},{3,4},{4,5},{5,6},{6,7},{7,8},{8,9},{9,10},{10,1... | collective-permute-start | bytes 249608 | tf_op jit(solution)/shard_map/ppermute | solution.py:25
  223.3 1.5 reshape.237
  224.8 1.5 reshape.248
  226.3 1.5 reshape.233
  227.8 1.9 collective-permute-start.3
  230.6 4.1 %collective-permute-done.3 = bf16[65,5,1,128]{3,2,1,0:T(2,128)(2,1)S(1)} collective-permute-done((bf16[65,5,1,128]{3,2,1,0:T(2,128)(2,1)}, bf16[65,5,1,128]{3,2,1,0:T(2,128)(2,1)S(1)}, u32[]{:S(2)}, u32[]{:S(2)}) %collective-permute-start.3) | collective-permute-done | bytes 83232 | tf_op jit(solution)/shard_map/ppermute | solution.py:27
  (113 shorter events, 29.6 us)
Async XLA Ops:
  0.6 80.0 %all-to-all-start = ((f32[4,16,768]{2,0,1:T(4,128)}), f32[4,16,768]{2,0,1:T(4,128)S(1)}, u32[]{:S(2)}, u32[]{:S(2)}) async-start(f32[4,16,768]{2,0,1:T(4,128)} %bitcast.252), calls=%async_computation | async-start | bytes 393216 | tf_op jit(solution)/shard_map/all_to_all | solution.py:77
  75.3 0.7 copy-start.10
  81.2 130.9 %collective-permute-start = (bf16[65,1,2,128]{3,2,1,0:T(2,128)(2,1)S(1)}, bf16[65,1,2,128]{3,2,1,0:T(2,128)(2,1)S(1)}, u32[]{:S(2)}, u32[]{:S(2)}) collective-permute-start(bf16[65,1,2,128]{3,2,1,0:T(2,128)(2,1)S(1)} %get-tuple-element.102), channel_id=1, source_target_pairs={{0,32},{32,64},{64,96},{96,128},{128,160},{160,192},{192,224},{224... | collective-permute-start | bytes 99848 | tf_op jit(solution)/shard_map/ppermute | solution.py:25
  84.5 127.7 %collective-permute-start.1 = (bf16[65,1,2,128]{3,2,1,0:T(2,128)(2,1)S(1)}, bf16[65,1,2,128]{3,2,1,0:T(2,128)(2,1)S(1)}, u32[]{:S(2)}, u32[]{:S(2)}) collective-permute-start(bf16[65,1,2,128]{3,2,1,0:T(2,128)(2,1)S(1)} %get-tuple-element.103), channel_id=1, source_target_pairs={{32,0},{64,32},{96,64},{128,96},{160,128},{192,160},{224,192},{256... | collective-permute-start | bytes 99848 | tf_op jit(solution)/shard_map/ppermute | solution.py:27
  199.1 1.7 copy-start
  213.3 16.4 %collective-permute-start.2 = (bf16[65,5,1,128]{3,2,1,0:T(2,128)(2,1)}, bf16[65,5,1,128]{3,2,1,0:T(2,128)(2,1)S(1)}, u32[]{:S(2)}, u32[]{:S(2)}) collective-permute-start(bf16[65,5,1,128]{3,2,1,0:T(2,128)(2,1)} %get-tuple-element.98), channel_id=1, source_target_pairs={{0,1},{1,2},{2,3},{3,4},{4,5},{5,6},{6,7},{7,8},{8,9},{9,10},{10,1... | collective-permute-start | bytes 249608 | tf_op jit(solution)/shard_map/ppermute | solution.py:25
  219.1 1.3 copy-start.5
  220.4 1.3 copy-start.6
  221.7 1.3 copy-start.7
  227.8 6.9 %collective-permute-start.3 = (bf16[65,5,1,128]{3,2,1,0:T(2,128)(2,1)}, bf16[65,5,1,128]{3,2,1,0:T(2,128)(2,1)S(1)}, u32[]{:S(2)}, u32[]{:S(2)}) collective-permute-start(bf16[65,5,1,128]{3,2,1,0:T(2,128)(2,1)} %get-tuple-element.99), channel_id=1, source_target_pairs={{1,0},{2,1},{3,2},{4,3},{5,4},{6,5},{7,6},{8,7},{9,8},{10,9},{11,1... | collective-permute-start | bytes 249608 | tf_op jit(solution)/shard_map/ppermute | solution.py:27
  230.5 5.1 %copy-start.4 = (bf16[65,6,8,128]{3,2,0,1:T(8,128)(2,1)S(1)}, bf16[65,6,8,128]{3,2,0,1:T(8,128)(2,1)}, u32[]{:S(2)}) copy-start(bf16[65,6,8,128]{3,2,0,1:T(8,128)(2,1)} %reshape.244) | copy-start | bytes 2396164
  235.4 1.1 copy-start.3
  235.6 1.5 copy-start.2
  236.6 1.2 copy-start.1
  238.8 1.0 copy-start.8
  239.8 0.8 copy-start.9
where the time goes:
time: 243 us; the launch traced here: 242 us
  blocking collectives  112 us (46%)
  other arithmetic  65.8 us (27%)
  local copies, waits for them, and re-layouts  18.6 us (8%)
  starting transfers between devices  17.4 us (7%)
  matrix products  16.2 us (7%)
  between operations  7.19 us (3%)
  waiting for transfers between devices  4.07 us (2%)
    psum x1, blocking collectives, per_device(): cov_sum, pixel_sum = lax.psum((partial_cov, pixel_total), ('chan', 'patch'))  112 us
    reduce_sum x11, other arithmetic, orthonormal_basis(): vector = vector - jnp.sum(earlier * vector) * earlier  32.4 us
    div x1, other arithmetic, orthonormal_basis(): columns.append(vector / jnp.sqrt(jnp.sum(vector * vector) + 1e-06))  18.4 us
    reshape x9, local copies, waits for them, and re-layouts, per_device(): binned = binned.reshape(NCH + 1, TA * TB, NBIN, TILE)  11.3 us
    dot_general x9, matrix products, per_device(): jnp.einsum('ctq,qk->ctk', centres, mask_table[offset_code], preferred_ele...  10.1 us
    all_to_all x1, starting transfers between devices, per_device(): lax.all_to_all(blocks, 'chan', split_axis=1, concat_axis=0, tiled=True)  7.6 us
    reduce_sum x4, other arithmetic, orthonormal_basis(): columns.append(vector / jnp.sqrt(jnp.sum(vector * vector) + 1e-06))  7.07 us
    ppermute x2, starting transfers between devices, padded(): lax.ppermute(tail, axis, [(i, (i + 1) % count) for i in range(ends)])  6.59 us
  transfers between devices with their start and end apart: 5, of which 1 were waited for; matrix products, arithmetic and copies ran while one was open for 38% of the time, Pallas kernels for 0%

commit v1 on v0

v1 whole, which is shorter than its diff:
```python
import functools
import math

import jax
import jax.numpy as jnp
from jax import lax
from jax.experimental import pallas as pl
from jax.experimental.pallas import tpu as pltpu
from jax.sharding import PartitionSpec as P

NCH = 64
MODES = 8
TILE = 128
NBIN = 8
NBR = 9
TA = 3
TB = 2
TILES = TA * TB
BLOCK = TILES * TILE
CORES = 2
F32 = jnp.float32
BF16 = jnp.bfloat16
HIGHEST = lax.Precision.HIGHEST
MESH = pl.DeviceIdType.MESH
NT = (((1,), (1,)), ((), ()))
SIDES = [(dk, dp) for dk in (-1, 0, 1) for dp in (-1, 0, 1) if (dk, dp) != (0, 0)]


def remote(src, dst, send, recv, chan, patch):
    return pltpu.make_async_remote_copy(
        src_ref=src,
        dst_ref=dst,
        send_sem=send,
        recv_sem=recv,
        device_id=(chan, patch),
        device_id_type=MESH,
    )


def span(step, extent):
    if step > 0:
        return pl.ds(extent, 1), pl.ds(0, 1)
    if step < 0:
        return pl.ds(1, 1), pl.ds(extent + 1, 1)
    return pl.ds(1, extent), pl.ds(1, extent)


def project_matrix(modes):
    lane = lax.broadcasted_iota(jnp.int32, (NCH, MODES), 1)
    for number in range(MODES):
        column = modes[:, number : number + 1]
        column = column / jnp.sqrt(jnp.sum(column * column, axis=0, keepdims=True) + 1e-06)
        inner = jnp.sum(modes * column, axis=0, keepdims=True)
        later = jnp.where(lane > number, modes - inner * column, modes)
        modes = jnp.where(lane == number, column, later)
    outer = lax.dot_general(modes, modes, NT, precision=HIGHEST, preferred_element_type=F32)
    return identity() - outer


def identity():
    rows = lax.broadcasted_iota(jnp.int32, (NCH, NCH), 0)
    cols = lax.broadcasted_iota(jnp.int32, (NCH, NCH), 1)
    return jnp.where(rows == cols, 1.0, 0.0).astype(F32)


def body(
    chans,
    patches,
    sky,
    modes,
    weight,
    nbr,
    cnt,
    bins,
    corr,
    cov_out,
    recv,
    w_own,
    w_left,
    w_right,
    table,
    mask,
    ext,
    cent,
    binned,
    w_binned,
    w_ext,
    w_part,
    acc,
    w_acc,
    piece,
    plane_in,
    z_out,
    z_in,
    whole_out,
    whole_in,
    packed_ref,
    local_sem,
    sky_send,
    sky_recv,
    w_send,
    w_recv,
    side_send,
    side_recv,
    plane_send,
    plane_recv,
    z_send,
    z_recv,
    whole_send,
    whole_recv,
):
    depth = patches // CORES
    plane = chans * CORES
    chan = lax.axis_index("chan")
    patch = lax.axis_index("patch")
    z = patch // CORES
    core = patch % CORES
    seat = chan * CORES + core

    def seat_device(other):
        return other // CORES, z * CORES + other % CORES

    def z_device(other):
        return chan, other * CORES + core

    table_copy = pltpu.make_async_copy(bins, table, local_sem.at[0])
    table_copy.start()
    weight_copy = pltpu.make_async_copy(weight, w_own, local_sem.at[1])
    weight_copy.start()

    def columns(other):
        return sky.at[:, pl.ds(pl.multiple_of(other * BLOCK, BLOCK), BLOCK)]

    own_copy = pltpu.make_async_copy(columns(chan), recv.at[chan], local_sem.at[2])
    own_copy.start()

    barrier = pltpu.get_barrier_semaphore()

    def greet(c, p):
        pl.semaphore_signal(barrier, inc=1, device_id=(c, p), device_id_type=MESH)

    @pl.loop(1, depth)
    def _(step):
        greet(*z_device((z + step) % depth))

    far = (patch + 2 * core - 1 + patches) % patches
    for shift in range(3):
        greet((chan + shift - 1 + chans) % chans, far)

    @pl.loop(1, plane)
    def _(step):
        greet(*seat_device((seat + step) % plane))

    pl.semaphore_wait(barrier, depth - 1 + 3 + plane - 1)

    def sky_copy(step):
        other = (chan + step) % chans
        return remote(
            columns(other), recv.at[chan], sky_send.at[step], sky_recv.at[step], other, patch
        )

    @pl.loop(1, chans)
    def _(step):
        sky_copy(step).start()

    right = (patch + 1) % patches
    left = (patch + patches - 1) % patches
    to_right = remote(weight, w_left, w_send.at[0], w_recv.at[0], chan, right)
    to_left = remote(weight, w_right, w_send.at[1], w_recv.at[1], chan, left)
    to_right.start()
    to_left.start()

    project = project_matrix(modes[...])

    table_copy.wait()

    @pl.loop(0, NBR)
    def _(code):
        bins_here = table[code]
        for level in range(NBIN):
            mask[code, :, level * TILE : (level + 1) * TILE] = jnp.where(
                bins_here == level, 1.0, 0.0
            ).astype(BF16)

    bits = []
    seen = []
    for a in range(TA):
        for b in range(TB):
            count = cnt[a, b]
            flags = jnp.int32(0)
            for slot in range(NBR):
                flags = flags + jnp.where(slot < count, jnp.int32(1) << nbr[a, b, slot], 0)
            bits.append(flags)
            seen.append(jnp.where(count > 0, 1.0, 0.0).astype(F32))

    weight_copy.wait()
    to_right.wait()
    to_left.wait()
    for row in range(TA + 2):
        tile_row = jnp.clip(chan * TA + row - 1, 0, chans * TA - 1)
        for col, (source, side) in enumerate(
            ((w_left, 1), (w_own, 0), (w_own, 1), (w_right, 0))
        ):
            w_ext[col, row] = source[tile_row * TB + side].astype(BF16).astype(F32)
    w_part[...] = jnp.zeros_like(w_part)
    for t in range(TILES):
        w_part[t : t + 1, :] = w_ext[1 + t % TB, 1 + t // TB]
    cent[TILES * NCH :, :] = w_part[...].astype(BF16)
    w_line = jnp.concatenate([w_own[chan * TILES + t] for t in range(TILES)], axis=1)
    acc[...] = jnp.zeros_like(acc)
    w_acc[...] = jnp.zeros_like(w_acc)

    own_copy.wait()

    @pl.loop(1, chans)
    def _(step):
        other = (chan + chans - step) % chans
        sky_copy(step).wait_send()
        remote(
            recv.at[other], recv.at[other], sky_send.at[step], sky_recv.at[step], other, patch
        ).wait_recv()

    gathered = recv[...].reshape(NCH, BLOCK)
    cleaned = lax.dot_general(
        project,
        gathered,
        (((1,), (0,)), ((), ())),
        precision=HIGHEST,
        preferred_element_type=F32,
    )
    weighted32 = cleaned * w_line
    weighted = weighted32.astype(BF16)
    for t in range(TILES):
        tile = weighted[:, t * TILE : (t + 1) * TILE]
        ext[1 + t % TB, 1 + t // TB] = tile
        cent[t * NCH : (t + 1) * NCH, :] = tile

    side_copies = []
    for number, (dk, dp) in enumerate(SIDES):
        row_src, row_dst = span(dk, TA)
        col_src, col_dst = span(dp, TB)
        copy = remote(
            ext.at[col_src, row_src],
            ext.at[col_dst, row_dst],
            side_send.at[number],
            side_recv.at[number],
            (chan + dk + chans) % chans,
            (patch + dp + patches) % patches,
        )
        copy.start()
        side_copies.append(copy)

    masked = jnp.concatenate(
        [
            (cent[t * NCH : (t + 1) * NCH, :].astype(F32) * seen[t]).astype(BF16)
            for t in range(TILES)
        ],
        axis=1,
    )
    part = lax.dot_general(masked, weighted, NT, preferred_element_type=F32)
    half = NCH // 2
    packed = jnp.concatenate([part[:half], part[half:]], axis=1)
    total = functools.reduce(lambda x, y: x + y, seen) * TILE
    for row in range(half):
        piece[row, 0:1, :] = packed[row : row + 1, :]
    piece[:, 1:2, :] = jnp.full((half, 1, TILE), total, F32)

    def plane_copy(step):
        other = (seat + step) % plane
        return remote(
            piece.at[other],
            plane_in.at[seat],
            plane_send.at[step],
            plane_recv.at[step],
            *seat_device(other),
        )

    @pl.loop(1, plane)
    def _(step):
        plane_copy(step).start()

    plane_in[seat] = piece[seat]

    @pl.loop(0, NBR)
    def _(code):
        centres = cent[...]
        for pair in range(NBIN // 2):
            lanes = slice(2 * pair * TILE, 2 * (pair + 1) * TILE)
            sums = jnp.dot(centres, mask[code, :, lanes], preferred_element_type=F32).astype(BF16)
            for half_bin in range(2):
                level = 2 * pair + half_bin
                cut = sums[:, half_bin * TILE : (half_bin + 1) * TILE]
                for t in range(TILES):
                    binned[
                        code,
                        level * NCH : (level + 1) * NCH,
                        t * TILE : (t + 1) * TILE,
                    ] = cut[t * NCH : (t + 1) * NCH, :]
                w_binned[code, :, level * TILE : (level + 1) * TILE] = cut[TILES * NCH :, :]

    @pl.loop(1, plane)
    def _(step):
        other = (seat + plane - step) % plane
        plane_copy(step).wait_send()
        remote(
            plane_in.at[other],
            plane_in.at[other],
            plane_send.at[step],
            plane_recv.at[step],
            *seat_device(other),
        ).wait_recv()

    plane_sum = jnp.sum(plane_in[...], axis=0)
    z_out[...] = plane_sum
    z_in[z] = plane_sum

    def z_copy(step):
        return remote(
            z_out, z_in.at[z], z_send.at[step], z_recv.at[step], *z_device((z + step) % depth)
        )

    @pl.loop(1, depth)
    def _(step):
        z_copy(step).start()

    for copy in side_copies:
        copy.wait()

    @pl.loop(0, NBR)
    def _(code):
        row_shift = code // 3
        col_shift = code % 3
        parts = []
        for t in range(TILES):
            present = ((bits[t] >> code) & 1).astype(F32)
            tile = ext[t % TB + col_shift, t // TB + row_shift]
            parts.append((tile.astype(F32) * present).astype(BF16))
            w_part[t : t + 1, :] = w_ext[t % TB + col_shift, t // TB + row_shift] * present
        partners = jnp.concatenate(parts, axis=1)
        acc[...] += lax.dot_general(binned[code], partners, NT, preferred_element_type=F32)
        w_tiles = w_part[0:8, :]
        w_acc[...] += w_binned[code].astype(F32)[0:8, :] * jnp.concatenate(
            [w_tiles] * NBIN, axis=1
        )

    @pl.loop(1, depth)
    def _(step):
        other = (z + depth - step) % depth
        z_copy(step).wait_send()
        remote(
            z_in.at[other], z_in.at[other], z_send.at[step], z_recv.at[step], *z_device(other)
        ).wait_recv()

    z_sum = jnp.sum(z_in[...], axis=0)
    whole_out[...] = z_sum
    whole_in[seat] = z_sum

    def whole_copy(step):
        return remote(
            whole_out,
            whole_in.at[seat],
            whole_send.at[step],
            whole_recv.at[step],
            *seat_device((seat + step) % plane),
        )

    @pl.loop(1, plane)
    def _(step):
        whole_copy(step).start()

    @pl.loop(1, plane)
    def _(step):
        other = (seat + plane - step) % plane
        whole_copy(step).wait_send()
        remote(
            whole_in.at[other],
            whole_in.at[other],
            whole_send.at[step],
            whole_recv.at[step],
            *seat_device(other),
        ).wait_recv()

    for row in range(half):
        packed_ref[row : row + 1, :] = whole_in[row, 0:1, :] / whole_in[row, 1:2, :]
    lines = packed_ref[...]
    covariance = jnp.concatenate([lines[:, :NCH], lines[:, NCH:]], axis=0)
    cov_out[...] = covariance
    only = covariance * identity()
    down = jnp.sqrt(jnp.sum(only, axis=1, keepdims=True) + 1e-06)
    across = jnp.sqrt(jnp.sum(only, axis=0, keepdims=True) + 1e-06)
    norm = down * across
    for level in range(NBIN):
        chunk = w_acc[:, level * TILE : (level + 1) * TILE]
        pairs = jnp.sum(jnp.sum(chunk, axis=0, keepdims=True), axis=1, keepdims=True)
        taper = 0.75 + 0.25 * math.cos(math.pi * level / NBIN)
        rows = acc[level * NCH : (level + 1) * NCH, :]
        corr[level] = taper * rows / (jnp.maximum(pairs, 1.0) * norm)


def per_device(sky_maps, mode_vectors, pixel_weight, neighbours, tile_counts, pair_bins):
    chans = lax.axis_size("chan")
    patches = lax.axis_size("patch")
    plane = chans * CORES
    depth = patches // CORES
    rows = chans * TILES
    weight = pixel_weight.reshape(rows, 1, TILE)
    dma = pltpu.SemaphoreType.DMA
    vmem = pltpu.VMEM
    anywhere = pl.BlockSpec(memory_space=pl.ANY)
    in_vmem = pl.BlockSpec(memory_space=pltpu.VMEM)
    in_smem = pl.BlockSpec(memory_space=pltpu.SMEM)
    correlation, covariance = pl.pallas_call(
        functools.partial(body, chans, patches),
        out_shape=(
            jax.ShapeDtypeStruct((NBIN, NCH, NCH), F32),
            jax.ShapeDtypeStruct((NCH, NCH), F32),
        ),
        in_specs=[anywhere, in_vmem, anywhere, in_smem, in_smem, anywhere],
        out_specs=(in_vmem, in_vmem),
        scratch_shapes=[
            vmem((chans, NCH // chans, BLOCK), F32),
            vmem((rows, 1, TILE), F32),
            vmem((rows, 1, TILE), F32),
            vmem((rows, 1, TILE), F32),
            vmem((NBR, TILE, TILE), jnp.int32),
            vmem((NBR, TILE, NBIN * TILE), BF16),
            vmem((TB + 2, TA + 2, NCH, TILE), BF16),
            vmem((TILES * NCH + 16, TILE), BF16),
            vmem((NBR, NBIN * NCH, BLOCK), BF16),
            vmem((NBR, 16, NBIN * TILE), BF16),
            vmem((TB + 2, TA + 2, 1, TILE), F32),
            vmem((16, TILE), F32),
            vmem((NBIN * NCH, NCH), F32),
            vmem((8, NBIN * TILE), F32),
            vmem((plane, 2, TILE), F32),
            vmem((plane, 2, TILE), F32),
            vmem((2, TILE), F32),
            vmem((depth, 2, TILE), F32),
            vmem((2, TILE), F32),
            vmem((plane, 2, TILE), F32),
            vmem((NCH // 2, TILE), F32),
            dma((3,)),
            dma((chans,)),
            dma((chans,)),
            dma((2,)),
            dma((2,)),
            dma((len(SIDES),)),
            dma((len(SIDES),)),
            dma((plane,)),
            dma((plane,)),
            dma((depth,)),
            dma((depth,)),
            dma((plane,)),
            dma((plane,)),
        ],
        compiler_params=pltpu.CompilerParams(collective_id=0, has_side_effects=True),
        name="sky_pairs",
    )(sky_maps, mode_vectors, weight, neighbours, tile_counts, pair_bins)
    return (correlation[None, None], covariance)


def solution(mesh):
    return jax.shard_map(
        per_device,
        mesh=mesh,
        in_specs=(
            P("chan", "patch"),
            P(),
            P("patch"),
            P("chan", "patch", None),
            P("chan", "patch"),
            P(),
        ),
        out_specs=(P("chan", "patch", None, None, None), P()),
        check_vma=False,
    )
```

time: 243 us -> 48.8 us (0.20)
  blocking collectives: 112 us -> 0 us
  other arithmetic: 65.8 us -> 0 us
  Pallas kernels: 0 us -> 43.5 us
  starting transfers between devices: 17.4 us -> 0 us
  matrix products: 16.2 us -> 0 us
  local copies, waits for them, and re-layouts: 18.6 us -> 4.34 us
  between operations: 7.19 us -> 0.66 us
  waiting for transfers between devices: 4.07 us -> 0 us
    psum x1 -> x0, blocking collectives: 112 us -> none  [per_device(): cov_sum, pixel_sum = lax.psum((partial_cov, pixel_total), ('chan', 'patch'))]
    pallas_call x0 -> x1, Pallas kernels: none -> 43.5 us  [per_device(): pl.pallas_call(functools.partial(body, chans, patches), out_shape=(jax.Sh...]
    reduce_sum x16 -> x0, other arithmetic: 40.8 us -> none  [the longest x11 32.4 us: orthonormal_basis(): vector = vector - jnp.sum(earlier * vector) * earlier]
    div x2 -> x0, other arithmetic: 19.1 us -> none  [the longest x1 18.4 us: orthonormal_basis(): columns.append(vector / jnp.sqrt(jnp.sum(vector * vector) + 1e-06))]
    dot_general x21 -> x0, matrix products: 16.2 us -> none  [the longest x9 10.1 us: per_device(): jnp.einsum('ctq,qk->ctk', centres, mask_table[offset_code], preferred_ele...]
    reshape x10 -> x0, local copies, waits for them, and re-layouts: 11.4 us -> none  [the longest x9 11.3 us: per_device(): binned = binned.reshape(NCH + 1, TA * TB, NBIN, TILE)]
    ppermute x4 -> x0, starting transfers between devices: 9.8 us -> none  [the longest x2 6.59 us: padded(): lax.ppermute(tail, axis, [(i, (i + 1) % count) for i in range(ends)])]
    all_to_all x1 -> x0, starting transfers between devices: 7.6 us -> none  [per_device(): lax.all_to_all(blocks, 'chan', split_axis=1, concat_axis=0, tiled=True)]
  transfers between devices with their start and end apart: 5 -> 0, of which waited for: 1 -> 0; matrix products, arithmetic and copies ran while one was open for 38% -> 0% of each run, Pallas kernels for 0% -> 0%
where the time goes in v1:
time: 48.8 us; the launch traced here: 48.5 us
  Pallas kernels  43.5 us (89%)
  local copies, waits for them, and re-layouts  4.34 us (9%)
  between operations  0.66 us (1%)
    pallas_call x1, Pallas kernels, per_device(): pl.pallas_call(functools.partial(body, chans, patches), out_shape=(jax.Sh...  43.5 us
    unnamed x8, local copies, waits for them, and re-layouts  4.34 us

profile of v1, /device:TPU:1, one launch (start us, length us, event | category | flops | bytes accessed | tf_op | source)
XLA Modules:
  0.0 48.5 jit_solution(14850915108557649580)
XLA Ops:
  0.6 0.0 copy-start.1
  0.6 1.3 %copy.9.cnt = s32[3,2]{1,0:T(4,128)} copy(s32[3,2]{0,1:T(2,128)} %param.10) | data formatting | bytes 48 | tf_op args[4]
  2.0 0.0 copy-done.1
  2.0 0.7 %copy.8.modes = f32[64,8]{1,0:T(8,128)} copy(f32[64,8]{0,1:T(8,128)S(1)} %copy-done.1) | data formatting | bytes 4096 | tf_op args[1]
  2.7 43.5 %sky_pairs.1 = (f32[8,64,64]{2,1,0:T(8,128)}, f32[64,64]{1,0:T(8,128)}) custom-call(f32[4,12288]{1,0:T(4,128)} %sky.1, f32[64,8]{1,0:T(8,128)} %copy.8.modes, f32[96,1,128]{2,1,0:T(1,128)} %bitcast.3, s32[3,2,9]{2,1,0:T(2,128)} %nbr.1, s32[3,2]{1,0:T(4,128)} %copy.9.cnt, s32[9,128,128]{2,1,0:T(8,128)} %bins.1), custom_call_target="tpu_custom_call" | custom-call | tf_op jit(solution)/shard_map/sky_pairs/pallas_call | solution.py:412
  46.2 0.0 copy-start
  46.2 1.7 %copy.12 = f32[1,1,8,64,64]{4,3,2,1,0:T(8,128)} copy(f32[1,1,8,64,64]{4,3,2,1,0:T(8,128)} %bitcast.2) | data formatting | bytes 262144
  47.9 0.0 copy-done
  47.9 0.6 %copy.13 = f32[64,64]{1,0:T(8,128)} copy(f32[64,64]{1,0:T(8,128)S(1)} %copy-done) | data formatting | bytes 32768
Async XLA Ops:
  0.6 1.4 %copy-start.1 = (f32[64,8]{0,1:T(8,128)S(1)}, f32[64,8]{0,1:T(8,128)}, u32[]{:S(2)}) copy-start(f32[64,8]{0,1:T(8,128)} %param.7) | copy-start | bytes 6148
  46.2 1.7 %copy-start = (f32[64,64]{1,0:T(8,128)S(1)}, f32[64,64]{1,0:T(8,128)}, u32[]{:S(2)}) copy-start(f32[64,64]{1,0:T(8,128)} %get-tuple-element.9) | copy-start | bytes 49156

commit v2 on v1

--- a/solution.py
+++ b/solution.py
@@ -75,6 +75,11 @@
     corr,
     cov_out,
     recv,
+    modes_in,
+    nbr_in,
+    cnt_in,
+    present,
+    seen,
     w_own,
     w_left,
     w_right,
@@ -108,60 +113,71 @@
     z_recv,
     whole_send,
     whole_recv,
+    ready,
 ):
     depth = patches // CORES
     plane = chans * CORES
+    side = math.isqrt(chans)
     chan = lax.axis_index("chan")
     patch = lax.axis_index("patch")
     z = patch // CORES
     core = patch % CORES
     seat = chan * CORES + core
-
-    def seat_device(other):
-        return other // CORES, z * CORES + other % CORES
+    chan_y = chan // side
+    chan_x = chan % side
+
+    shifts = [(dy, dx) for dy in range(side) for dx in range(side)]
+    shifts.sort(key=lambda d: -(min(d[0], side - d[0]) + min(d[1], side - d[1])))
+    ahead = [(chan_y + dy) % side * side + (chan_x + dx) % side for dy, dx in shifts]
+    behind = [
+        (chan_y + side - dy) % side * side + (chan_x + side - dx) % side for dy, dx in shifts
+    ]
+    cores = (core, 1 - core)
+    seats = [(i, c) for i in range(chans) for c in range(CORES) if (i, c) != (chans - 1, 0)]
 
     def z_device(other):
         return chan, other * CORES + core
 
-    table_copy = pltpu.make_async_copy(bins, table, local_sem.at[0])
-    table_copy.start()
-    weight_copy = pltpu.make_async_copy(weight, w_own, local_sem.at[1])
-    weight_copy.start()
+    def signal(semaphore, device):
+        pl.semaphore_signal(semaphore, inc=1, device_id=device, device_id_type=MESH)
+
+    barrier = pltpu.get_barrier_semaphore()
+    far = (patch + 2 * core - 1 + patches) % patches
+    for shift in range(3):
+        signal(barrier, ((chan + shift - 1 + chans) % chans, far))
+    for i, c in seats:
+        signal(barrier, (ahead[i], z * CORES + cores[c]))
+    signal(barrier, z_device((z + 1) % depth))
+    signal(barrier, z_device((z + depth - 1) % depth))
 
     def columns(other):
         return sky.at[:, pl.ds(pl.multiple_of(other * BLOCK, BLOCK), BLOCK)]
 
-    own_copy = pltpu.make_async_copy(columns(chan), recv.at[chan], local_sem.at[2])
-    own_copy.start()
-
-    barrier = pltpu.get_barrier_semaphore()
-
-    def greet(c, p):
-        pl.semaphore_signal(barrier, inc=1, device_id=(c, p), device_id_type=MESH)
-
-    @pl.loop(1, depth)
-    def _(step):
-        greet(*z_device((z + step) % depth))
-
-    far = (patch + 2 * core - 1 + patches) % patches
-    for shift in range(3):
-        greet((chan + shift - 1 + chans) % chans, far)
-
-    @pl.loop(1, plane)
-    def _(step):
-        greet(*seat_device((seat + step) % plane))
-
-    pl.semaphore_wait(barrier, depth - 1 + 3 + plane - 1)
-
-    def sky_copy(step):
-        other = (chan + step) % chans
+    local_copies = [
+        pltpu.make_async_copy(source, target, local_sem.at[number])
+        for number, (source, target) in enumerate(
+            (
+                (modes, modes_in),
+                (bins, table),
+                (nbr, nbr_in),
+                (cnt, cnt_in),
+                (weight, w_own),
+                (columns(chan), recv.at[chan]),
+            )
+        )
+    ]
+    for copy in local_copies:
+        copy.start()
+
+    pl.semaphore_wait(barrier, 3 + len(seats) + 2)
+
+    def sky_copy(i):
         return remote(
-            columns(other), recv.at[chan], sky_send.at[step], sky_recv.at[step], other, patch
-        )
-
-    @pl.loop(1, chans)
-    def _(step):
-        sky_copy(step).start()
+            columns(ahead[i]), recv.at[chan], sky_send.at[i], sky_recv.at[i], ahead[i], patch
+        )
+
+    for i in range(chans - 1):
+        sky_copy(i).start()
 
     right = (patch + 1) % patches
     left = (patch + patches - 1) % patches
@@ -170,9 +186,22 @@
     to_right.start()
     to_left.start()
 
-    project = project_matrix(modes[...])
-
-    table_copy.wait()
+    reaches = [1 << r for r in range((depth // 2).bit_length() - 1)]
+
+    def announce(r):
+        signal(ready.at[r], z_device((z + reaches[r]) % depth))
+        signal(ready.at[r], z_device((z + depth - reaches[r]) % depth))
+
+    def hear(r):
+        pl.semaphore_wait(ready.at[r], 2)
+
+    announce(0)
+    for copy in local_copies[:-1]:
+        copy.wait()
+
+    project = project_matrix(modes_in[...].T)
+    hear(0)
+    announce(1)
 
     @pl.loop(0, NBR)
     def _(code):
@@ -182,18 +211,22 @@
                 bins_here == level, 1.0, 0.0
             ).astype(BF16)
 
-    bits = []
-    seen = []
+    slots = lax.broadcasted_iota(jnp.int32, (TB, NBR), 1)
     for a in range(TA):
+        count = cnt_in[:, a : a + 1]
+        live = jnp.where(slots < count, nbr_in[a], NBR)
+        observed = jnp.broadcast_to(jnp.where(count > 0, 1.0, 0.0).astype(F32), (TB, TILE))
         for b in range(TB):
-            count = cnt[a, b]
-            flags = jnp.int32(0)
-            for slot in range(NBR):
-                flags = flags + jnp.where(slot < count, jnp.int32(1) << nbr[a, b, slot], 0)
-            bits.append(flags)
-            seen.append(jnp.where(count > 0, 1.0, 0.0).astype(F32))
-
-    weight_copy.wait()
+            seen[a * TB + b] = observed[b : b + 1, :]
+        for code in range(NBR):
+            hit = jnp.max(jnp.where(live == code, 1.0, 0.0).astype(F32), axis=1, keepdims=True)
+            hit = jnp.broadcast_to(hit, (TB, TILE))
+            for b in range(TB):
+                present[code, a * TB + b] = hit[b : b + 1, :]
+    for r in range(1, len(reaches) - 1):
+        hear(r)
+        announce(r + 1)
+
     to_right.wait()
     to_left.wait()
     for row in range(TA + 2):
@@ -210,14 +243,16 @@
     acc[...] = jnp.zeros_like(acc)
     w_acc[...] = jnp.zeros_like(w_acc)
 
-    own_copy.wait()
-
-    @pl.loop(1, chans)
-    def _(step):
-        other = (chan + chans - step) % chans
-        sky_copy(step).wait_send()
+    local_copies[-1].wait()
+    for i in range(chans - 1):
+        sky_copy(i).wait_send()
         remote(
-            recv.at[other], recv.at[other], sky_send.at[step], sky_recv.at[step], other, patch
+            recv.at[behind[i]],
+            recv.at[behind[i]],
+            sky_send.at[i],
+            sky_recv.at[i],
+            behind[i],
+            patch,
         ).wait_recv()
 
     gathered = recv[...].reshape(NCH, BLOCK)
@@ -260,24 +295,35 @@
     part = lax.dot_general(masked, weighted, NT, preferred_element_type=F32)
     half = NCH // 2
     packed = jnp.concatenate([part[:half], part[half:]], axis=1)
-    total = functools.reduce(lambda x, y: x + y, seen) * TILE
+    total = jnp.sum(seen[...], axis=0) * TILE
     for row in range(half):
         piece[row, 0:1, :] = packed[row : row + 1, :]
-    piece[:, 1:2, :] = jnp.full((half, 1, TILE), total, F32)
-
-    def plane_copy(step):
-        other = (seat + step) % plane
-        return remote(
-            piece.at[other],
-            plane_in.at[seat],
-            plane_send.at[step],
-            plane_recv.at[step],
-            *seat_device(other),
-        )
-
-    @pl.loop(1, plane)
-    def _(step):
-        plane_copy(step).start()
+    piece[:, 1:2, :] = jnp.broadcast_to(total[None], (half, 1, TILE))
+
+    def seat_of(chan_list, n):
+        i, c = seats[n]
+        return chan_list[i] * CORES + cores[c]
+
+    def plane_start(n, source, target, send, recv_sem):
+        i, c = seats[n]
+        copy = remote(
+            source, target, send.at[n], recv_sem.at[n], ahead[i], z * CORES + cores[c]
+        )
+        copy.start()
+        return copy
+
+    def plane_wait(n, sent, target, send, recv_sem):
+        i, c = seats[n]
+        slot = target.at[seat_of(behind, n)]
+        sent.wait_send()
+        remote(
+            slot, slot, send.at[n], recv_sem.at[n], behind[i], z * CORES + cores[c]
+        ).wait_recv()
+
+    plane_copies = [
+        plane_start(n, piece.at[seat_of(ahead, n)], plane_in.at[seat], plane_send, plane_recv)
+        for n in range(len(seats))
+    ]
 
     plane_in[seat] = piece[seat]
 
@@ -298,17 +344,8 @@
                     ] = cut[t * NCH : (t + 1) * NCH, :]
                 w_binned[code, :, level * TILE : (level + 1) * TILE] = cut[TILES * NCH :, :]
 
-    @pl.loop(1, plane)
-    def _(step):
-        other = (seat + plane - step) % plane
-        plane_copy(step).wait_send()
-        remote(
-            plane_in.at[other],
-            plane_in.at[other],
-            plane_send.at[step],
-            plane_recv.at[step],
-            *seat_device(other),
-        ).wait_recv()
+    for n in range(len(seats)):
+        plane_wait(n, plane_copies[n], plane_in, plane_send, plane_recv)
 
     plane_sum = jnp.sum(plane_in[...], axis=0)
     z_out[...] = plane_sum
@@ -318,6 +355,8 @@
         return remote(
             z_out, z_in.at[z], z_send.at[step], z_recv.at[step], *z_device((z + step) % depth)
         )
+
+    hear(len(reaches) - 1)
 
     @pl.loop(1, depth)
     def _(step):
@@ -332,10 +371,10 @@
         col_shift = code % 3
         parts = []
         for t in range(TILES):
-            present = ((bits[t] >> code) & 1).astype(F32)
+            here = present[code, t]
             tile = ext[t % TB + col_shift, t // TB + row_shift]
-            parts.append((tile.astype(F32) * present).astype(BF16))
-            w_part[t : t + 1, :] = w_ext[t % TB + col_shift, t // TB + row_shift] * present
+            parts.append((tile.astype(F32) * here).astype(BF16))
+            w_part[t : t + 1, :] = w_ext[t % TB + col_shift, t // TB + row_shift] * here
         partners = jnp.concatenate(parts, axis=1)
         acc[...] += lax.dot_general(binned[code], partners, NT, preferred_element_type=F32)
         w_tiles = w_part[0:8, :]
@@ -355,30 +394,18 @@
     whole_out[...] = z_sum
     whole_in[seat] = z_sum
 
-    def whole_copy(step):
-        return remote(
-            whole_out,
-            whole_in.at[seat],
-            whole_send.at[step],
-            whole_recv.at[step],
-            *seat_device((seat + step) % plane),
-        )
-
-    @pl.loop(1, plane)
-    def _(step):
-        whole_copy(step).start()
-
-    @pl.loop(1, plane)
-    def _(step):
-        other = (seat + plane - step) % plane
-        whole_copy(step).wait_send()
-        remote(
-            whole_in.at[other],
-            whole_in.at[other],
-            whole_send.at[step],
-            whole_recv.at[step],
-            *seat_device(other),
-        ).wait_recv()
+    whole_copies = [
+        plane_start(n, whole_out, whole_in.at[seat], whole_send, whole_recv)
+        for n in range(len(seats))
+    ]
+    scales = []
+    for level in range(NBIN):
+        chunk = w_acc[:, level * TILE : (level + 1) * TILE]
+        scales.append(
+            jnp.maximum(jnp.sum(jnp.sum(chunk, axis=0, keepdims=True), axis=1, keepdims=True), 1.0)
+        )
+    for n in range(len(seats)):
+        plane_wait(n, whole_copies[n], whole_in, whole_send, whole_recv)
 
     for row in range(half):
         packed_ref[row : row + 1, :] = whole_in[row, 0:1, :] / whole_in[row, 1:2, :]
@@ -390,11 +417,9 @@
     across = jnp.sqrt(jnp.sum(only, axis=0, keepdims=True) + 1e-06)
     norm = down * across
     for level in range(NBIN):
-        chunk = w_acc[:, level * TILE : (level + 1) * TILE]
-        pairs = jnp.sum(jnp.sum(chunk, axis=0, keepdims=True), axis=1, keepdims=True)
         taper = 0.75 + 0.25 * math.cos(math.pi * level / NBIN)
         rows = acc[level * NCH : (level + 1) * NCH, :]
-        corr[level] = taper * rows / (jnp.maximum(pairs, 1.0) * norm)
+        corr[level] = taper * rows / (scales[level] * norm)
 
 
 def per_device(sky_maps, mode_vectors, pixel_weight, neighbours, tile_counts, pair_bins):
@@ -408,17 +433,21 @@
     vmem = pltpu.VMEM
     anywhere = pl.BlockSpec(memory_space=pl.ANY)
     in_vmem = pl.BlockSpec(memory_space=pltpu.VMEM)
-    in_smem = pl.BlockSpec(memory_space=pltpu.SMEM)
     correlation, covariance = pl.pallas_call(
         functools.partial(body, chans, patches),
         out_shape=(
             jax.ShapeDtypeStruct((NBIN, NCH, NCH), F32),
             jax.ShapeDtypeStruct((NCH, NCH), F32),
         ),
-        in_specs=[anywhere, in_vmem, anywhere, in_smem, in_smem, anywhere],
+        in_specs=[anywhere] * 6,
         out_specs=(in_vmem, in_vmem),
         scratch_shapes=[
             vmem((chans, NCH // chans, BLOCK), F32),
+            vmem((MODES, NCH), F32),
+            vmem((TA, TB, NBR), jnp.int32),
+            vmem((TB, TA), jnp.int32),
+            vmem((NBR, TILES, 1, TILE), F32),
+            vmem((TILES, 1, TILE), F32),
             vmem((rows, 1, TILE), F32),
             vmem((rows, 1, TILE), F32),
             vmem((rows, 1, TILE), F32),
@@ -439,7 +468,7 @@
             vmem((2, TILE), F32),
             vmem((plane, 2, TILE), F32),
             vmem((NCH // 2, TILE), F32),
-            dma((3,)),
+            dma((6,)),
             dma((chans,)),
             dma((chans,)),
             dma((2,)),
@@ -452,10 +481,11 @@
             dma((depth,)),
             dma((plane,)),
             dma((plane,)),
+            pltpu.SemaphoreType.REGULAR((max(1, (depth // 2).bit_length() - 1),)),
         ],
         compiler_params=pltpu.CompilerParams(collective_id=0, has_side_effects=True),
         name="sky_pairs",
-    )(sky_maps, mode_vectors, weight, neighbours, tile_counts, pair_bins)
+    )(sky_maps, mode_vectors.T, weight, neighbours, tile_counts.T, pair_bins)
     return (correlation[None, None], covariance)
 
 

time: 48.8 us -> 44.5 us (0.912)
  Pallas kernels: 43.5 us -> 41.4 us
  local copies, waits for them, and re-layouts: 4.34 us -> 2.3 us
    pallas_call x1, Pallas kernels: 43.5 us -> 41.4 us  [per_device(): pl.pallas_call(functools.partial(body, chans, patches), out_shape=(jax.Sh...]
    unnamed x8 -> x4, local copies, waits for them, and re-layouts: 4.34 us -> 2.3 us
where the time goes in v2:
time: 44.5 us; the launch traced here: 44.4 us
  Pallas kernels  41.4 us (93%)
  local copies, waits for them, and re-layouts  2.3 us (5%)
  between operations  0.65 us (1%)
    pallas_call x1, Pallas kernels, per_device(): pl.pallas_call(functools.partial(body, chans, patches), out_shape=(jax.Sh...  41.4 us
    unnamed x4, local copies, waits for them, and re-layouts  2.3 us

profile of v2, /device:TPU:1, one launch (start us, length us, event | category | flops | bytes accessed | tf_op | source)
XLA Modules:
  0.0 44.4 jit_solution(2951799113978293020)
XLA Ops:
  0.6 41.4 %sky_pairs.1 = (f32[8,64,64]{2,1,0:T(8,128)}, f32[64,64]{1,0:T(8,128)}) custom-call(f32[4,12288]{1,0:T(4,128)} %sky.1, f32[8,64]{1,0:T(8,128)} %bitcast.6, f32[96,1,128]{2,1,0:T(1,128)} %bitcast.5, s32[3,2,9]{2,1,0:T(2,128)} %nbr.1, s32[2,3]{1,0:T(2,128)} %bitcast.7, s32[9,128,128]{2,1,0:T(8,128)} %bins.1), custom_call_target="tpu_custom_call" | custom-call | tf_op jit(solution)/shard_map/sky_pairs/pallas_call | solution.py:436
  42.1 0.0 copy-start
  42.1 1.7 %copy.10 = f32[1,1,8,64,64]{4,3,2,1,0:T(8,128)} copy(f32[1,1,8,64,64]{4,3,2,1,0:T(8,128)} %bitcast.4) | data formatting | bytes 262144
  43.8 0.0 copy-done
  43.8 0.6 %copy.11 = f32[64,64]{1,0:T(8,128)} copy(f32[64,64]{1,0:T(8,128)S(1)} %copy-done) | data formatting | bytes 32768
Async XLA Ops:
  42.1 1.7 %copy-start = (f32[64,64]{1,0:T(8,128)S(1)}, f32[64,64]{1,0:T(8,128)}, u32[]{:S(2)}) copy-start(f32[64,64]{1,0:T(8,128)} %get-tuple-element.9) | copy-start | bytes 49156

commit v3 on v2

--- a/solution.py
+++ b/solution.py
@@ -75,6 +75,7 @@
     corr,
     cov_out,
     recv,
+    sky_in,
     modes_in,
     nbr_in,
     cnt_in,
@@ -151,7 +152,7 @@
     signal(barrier, z_device((z + depth - 1) % depth))
 
     def columns(other):
-        return sky.at[:, pl.ds(pl.multiple_of(other * BLOCK, BLOCK), BLOCK)]
+        return sky_in.at[:, pl.ds(pl.multiple_of(other * BLOCK, BLOCK), BLOCK)]
 
     local_copies = [
         pltpu.make_async_copy(source, target, local_sem.at[number])
@@ -162,13 +163,14 @@
                 (nbr, nbr_in),
                 (cnt, cnt_in),
                 (weight, w_own),
-                (columns(chan), recv.at[chan]),
+                (sky, sky_in),
             )
         )
     ]
     for copy in local_copies:
         copy.start()
 
+    local_copies[-1].wait()
     pl.semaphore_wait(barrier, 3 + len(seats) + 2)
 
     def sky_copy(i):
@@ -196,6 +198,7 @@
         pl.semaphore_wait(ready.at[r], 2)
 
     announce(0)
+    recv[chan] = sky_in[:, pl.ds(pl.multiple_of(chan * BLOCK, BLOCK), BLOCK)]
     for copy in local_copies[:-1]:
         copy.wait()
 
@@ -243,7 +246,6 @@
     acc[...] = jnp.zeros_like(acc)
     w_acc[...] = jnp.zeros_like(w_acc)
 
-    local_copies[-1].wait()
     for i in range(chans - 1):
         sky_copy(i).wait_send()
         remote(
@@ -265,6 +267,44 @@
     )
     weighted32 = cleaned * w_line
     weighted = weighted32.astype(BF16)
+    masked = jnp.concatenate(
+        [weighted32[:, t * TILE : (t + 1) * TILE] * seen[t] for t in range(TILES)], axis=1
+    ).astype(BF16)
+    part = lax.dot_general(masked, weighted, NT, preferred_element_type=F32)
+    half = NCH // 2
+    packed = jnp.concatenate([part[:half], part[half:]], axis=1)
+    total = jnp.sum(seen[...], axis=0) * TILE
+    for row in range(half):
+        piece[row, 0:1, :] = packed[row : row + 1, :]
+    piece[:, 1:2, :] = jnp.broadcast_to(total[None], (half, 1, TILE))
+
+    def seat_of(chan_list, n):
+        i, c = seats[n]
+        return chan_list[i] * CORES + cores[c]
+
+    def plane_start(n, source, target, send, recv_sem):
+        i, c = seats[n]
+        copy = remote(
+            source, target, send.at[n], recv_sem.at[n], ahead[i], z * CORES + cores[c]
+        )
+        copy.start()
+        return copy
+
+    def plane_wait(n, sent, target, send, recv_sem):
+        i, c = seats[n]
+        slot = target.at[seat_of(behind, n)]
+        sent.wait_send()
+        remote(
+            slot, slot, send.at[n], recv_sem.at[n], behind[i], z * CORES + cores[c]
+        ).wait_recv()
+
+    plane_copies = [
+        plane_start(n, piece.at[seat_of(ahead, n)], plane_in.at[seat], plane_send, plane_recv)
+        for n in range(len(seats))
+    ]
+
+    plane_in[seat] = piece[seat]
+
     for t in range(TILES):
         tile = weighted[:, t * TILE : (t + 1) * TILE]
         ext[1 + t % TB, 1 + t // TB] = tile
@@ -285,47 +325,6 @@
         copy.start()
         side_copies.append(copy)
 
-    masked = jnp.concatenate(
-        [
-            (cent[t * NCH : (t + 1) * NCH, :].astype(F32) * seen[t]).astype(BF16)
-            for t in range(TILES)
-        ],
-        axis=1,
-    )
-    part = lax.dot_general(masked, weighted, NT, preferred_element_type=F32)
-    half = NCH // 2
-    packed = jnp.concatenate([part[:half], part[half:]], axis=1)
-    total = jnp.sum(seen[...], axis=0) * TILE
-    for row in range(half):
-        piece[row, 0:1, :] = packed[row : row + 1, :]
-    piece[:, 1:2, :] = jnp.broadcast_to(total[None], (half, 1, TILE))
-
-    def seat_of(chan_list, n):
-        i, c = seats[n]
-        return chan_list[i] * CORES + cores[c]
-
-    def plane_start(n, source, target, send, recv_sem):
-        i, c = seats[n]
-        copy = remote(
-            source, target, send.at[n], recv_sem.at[n], ahead[i], z * CORES + cores[c]
-        )
-        copy.start()
-        return copy
-
-    def plane_wait(n, sent, target, send, recv_sem):
-        i, c = seats[n]
-        slot = target.at[seat_of(behind, n)]
-        sent.wait_send()
-        remote(
-            slot, slot, send.at[n], recv_sem.at[n], behind[i], z * CORES + cores[c]
-        ).wait_recv()
-
-    plane_copies = [
-        plane_start(n, piece.at[seat_of(ahead, n)], plane_in.at[seat], plane_send, plane_recv)
-        for n in range(len(seats))
-    ]
-
-    plane_in[seat] = piece[seat]
 
     @pl.loop(0, NBR)
     def _(code):
@@ -351,16 +350,16 @@
     z_out[...] = plane_sum
     z_in[z] = plane_sum
 
-    def z_copy(step):
-        return remote(
-            z_out, z_in.at[z], z_send.at[step], z_recv.at[step], *z_device((z + step) % depth)
-        )
-
+    steps = sorted(range(1, depth), key=lambda d: -min(d, depth - d))
     hear(len(reaches) - 1)
-
-    @pl.loop(1, depth)
-    def _(step):
-        z_copy(step).start()
+    z_copies = [
+        remote(
+            z_out, z_in.at[z], z_send.at[d], z_recv.at[d], *z_device((z + d) % depth)
+        )
+        for d in steps
+    ]
+    for copy in z_copies:
+        copy.start()
 
     for copy in side_copies:
         copy.wait()
@@ -382,12 +381,11 @@
             [w_tiles] * NBIN, axis=1
         )
 
-    @pl.loop(1, depth)
-    def _(step):
-        other = (z + depth - step) % depth
-        z_copy(step).wait_send()
+    for d, copy in zip(steps, z_copies):
+        other = (z + depth - d) % depth
+        copy.wait_send()
         remote(
-            z_in.at[other], z_in.at[other], z_send.at[step], z_recv.at[step], *z_device(other)
+            z_in.at[other], z_in.at[other], z_send.at[d], z_recv.at[d], *z_device(other)
         ).wait_recv()
 
     z_sum = jnp.sum(z_in[...], axis=0)
@@ -436,13 +434,14 @@
     correlation, covariance = pl.pallas_call(
         functools.partial(body, chans, patches),
         out_shape=(
-            jax.ShapeDtypeStruct((NBIN, NCH, NCH), F32),
-            jax.ShapeDtypeStruct((NCH, NCH), F32),
+            pltpu.VMEM((NBIN, NCH, NCH), F32),
+            pltpu.VMEM((NCH, NCH), F32),
         ),
         in_specs=[anywhere] * 6,
         out_specs=(in_vmem, in_vmem),
         scratch_shapes=[
             vmem((chans, NCH // chans, BLOCK), F32),
+            vmem((NCH // chans, chans * BLOCK), F32),
             vmem((MODES, NCH), F32),
             vmem((TA, TB, NBR), jnp.int32),
             vmem((TB, TA), jnp.int32),

time: 44.5 us -> 42.1 us (0.946)
  Pallas kernels: 41.4 us -> 40 us
  local copies, waits for them, and re-layouts: 2.3 us -> 1.32 us
    pallas_call x1, Pallas kernels: 41.4 us -> 40 us  [per_device(): pl.pallas_call(functools.partial(body, chans, patches), out_shape=(pltpu....]
    unnamed x4 -> x2, local copies, waits for them, and re-layouts: 2.3 us -> 1.32 us
where the time goes in v3:
time: 42.1 us; the launch traced here: 42 us
  Pallas kernels  40 us (95%)
  local copies, waits for them, and re-layouts  1.32 us (3%)
  between operations  0.64 us (2%)
    pallas_call x1, Pallas kernels, per_device(): pl.pallas_call(functools.partial(body, chans, patches), out_shape=(pltpu....  40 us
    unnamed x2, local copies, waits for them, and re-layouts  1.32 us

profile of v3, /device:TPU:1, one launch (start us, length us, event | category | flops | bytes accessed | tf_op | source)
XLA Modules:
  0.0 42.0 jit_solution(1136903862245313961)
XLA Ops:
  0.6 40.0 %sky_pairs.1 = (f32[8,64,64]{2,1,0:T(8,128)S(1)}, f32[64,64]{1,0:T(8,128)S(1)}) custom-call(f32[4,12288]{1,0:T(4,128)} %sky.1, f32[8,64]{1,0:T(8,128)} %bitcast.6, f32[96,1,128]{2,1,0:T(1,128)} %bitcast.5, s32[3,2,9]{2,1,0:T(2,128)} %nbr.1, s32[2,3]{1,0:T(2,128)} %bitcast.7, s32[9,128,128]{2,1,0:T(8,128)} %bins.1), custom_call_target="tpu_custom_call" | custom-call | tf_op jit(solution)/shard_map/sky_pairs/pallas_call | solution.py:434
  40.7 0.7 %copy.10 = f32[1,1,8,64,64]{4,3,2,1,0:T(8,128)} copy(f32[1,1,8,64,64]{4,3,2,1,0:T(8,128)S(1)} %bitcast.4) | data formatting | bytes 262144
  41.4 0.6 %copy.11 = f32[64,64]{1,0:T(8,128)} copy(f32[64,64]{1,0:T(8,128)S(1)} %get-tuple-element.7) | data formatting | bytes 32768

commit v4 on v3

--- a/solution.py
+++ b/solution.py
@@ -234,10 +234,10 @@
     to_left.wait()
     for row in range(TA + 2):
         tile_row = jnp.clip(chan * TA + row - 1, 0, chans * TA - 1)
-        for col, (source, side) in enumerate(
+        for col, (source, edge) in enumerate(
             ((w_left, 1), (w_own, 0), (w_own, 1), (w_right, 0))
         ):
-            w_ext[col, row] = source[tile_row * TB + side].astype(BF16).astype(F32)
+            w_ext[col, row] = source[tile_row * TB + edge].astype(BF16).astype(F32)
     w_part[...] = jnp.zeros_like(w_part)
     for t in range(TILES):
         w_part[t : t + 1, :] = w_ext[1 + t % TB, 1 + t // TB]
@@ -272,15 +272,23 @@
     ).astype(BF16)
     part = lax.dot_general(masked, weighted, NT, preferred_element_type=F32)
     half = NCH // 2
+    pieces = side * CORES
+    lines = half // pieces
     packed = jnp.concatenate([part[:half], part[half:]], axis=1)
     total = jnp.sum(seen[...], axis=0) * TILE
-    for row in range(half):
-        piece[row, 0:1, :] = packed[row : row + 1, :]
-    piece[:, 1:2, :] = jnp.broadcast_to(total[None], (half, 1, TILE))
+    for number in range(pieces):
+        piece[number, 0:lines, :] = packed[number * lines : (number + 1) * lines, :]
+        piece[number, lines : lines + 1, :] = total
 
     def seat_of(chan_list, n):
         i, c = seats[n]
         return chan_list[i] * CORES + cores[c]
+
+    def piece_of(chan_list, n):
+        i, c = seats[n]
+        return chan_list[i] % side * CORES + cores[c]
+
+    own_piece = chan_x * CORES + core
 
     def plane_start(n, source, target, send, recv_sem):
         i, c = seats[n]
@@ -290,20 +298,20 @@
         copy.start()
         return copy
 
-    def plane_wait(n, sent, target, send, recv_sem):
+    def plane_wait(n, sent, target, slot_of, send, recv_sem):
         i, c = seats[n]
-        slot = target.at[seat_of(behind, n)]
+        slot = target.at[slot_of(behind, n)]
         sent.wait_send()
         remote(
             slot, slot, send.at[n], recv_sem.at[n], behind[i], z * CORES + cores[c]
         ).wait_recv()
 
     plane_copies = [
-        plane_start(n, piece.at[seat_of(ahead, n)], plane_in.at[seat], plane_send, plane_recv)
+        plane_start(n, piece.at[piece_of(ahead, n)], plane_in.at[seat], plane_send, plane_recv)
         for n in range(len(seats))
     ]
 
-    plane_in[seat] = piece[seat]
+    plane_in[seat] = piece[own_piece]
 
     for t in range(TILES):
         tile = weighted[:, t * TILE : (t + 1) * TILE]
@@ -344,7 +352,7 @@
                 w_binned[code, :, level * TILE : (level + 1) * TILE] = cut[TILES * NCH :, :]
 
     for n in range(len(seats)):
-        plane_wait(n, plane_copies[n], plane_in, plane_send, plane_recv)
+        plane_wait(n, plane_copies[n], plane_in, seat_of, plane_send, plane_recv)
 
     plane_sum = jnp.sum(plane_in[...], axis=0)
     z_out[...] = plane_sum
@@ -390,11 +398,12 @@
 
     z_sum = jnp.sum(z_in[...], axis=0)
     whole_out[...] = z_sum
-    whole_in[seat] = z_sum
-
+    whole_in[own_piece] = z_sum
+
+    row_seats = [n for n, (i, c) in enumerate(seats) if shifts[i][0] == 0]
     whole_copies = [
-        plane_start(n, whole_out, whole_in.at[seat], whole_send, whole_recv)
-        for n in range(len(seats))
+        plane_start(n, whole_out, whole_in.at[own_piece], whole_send, whole_recv)
+        for n in row_seats
     ]
     scales = []
     for level in range(NBIN):
@@ -402,13 +411,15 @@
         scales.append(
             jnp.maximum(jnp.sum(jnp.sum(chunk, axis=0, keepdims=True), axis=1, keepdims=True), 1.0)
         )
-    for n in range(len(seats)):
-        plane_wait(n, whole_copies[n], whole_in, whole_send, whole_recv)
-
-    for row in range(half):
-        packed_ref[row : row + 1, :] = whole_in[row, 0:1, :] / whole_in[row, 1:2, :]
-    lines = packed_ref[...]
-    covariance = jnp.concatenate([lines[:, :NCH], lines[:, NCH:]], axis=0)
+    for n, copy in zip(row_seats, whole_copies):
+        plane_wait(n, copy, whole_in, piece_of, whole_send, whole_recv)
+
+    for number in range(pieces):
+        packed_ref[number * lines : (number + 1) * lines, :] = (
+            whole_in[number, 0:lines, :] / whole_in[number, lines : lines + 1, :]
+        )
+    merged = packed_ref[...]
+    covariance = jnp.concatenate([merged[:, :NCH], merged[:, NCH:]], axis=0)
     cov_out[...] = covariance
     only = covariance * identity()
     down = jnp.sqrt(jnp.sum(only, axis=1, keepdims=True) + 1e-06)
@@ -426,6 +437,8 @@
     plane = chans * CORES
     depth = patches // CORES
     rows = chans * TILES
+    pieces = math.isqrt(chans) * CORES
+    lines = NCH // 2 // pieces + 1
     weight = pixel_weight.reshape(rows, 1, TILE)
     dma = pltpu.SemaphoreType.DMA
     vmem = pltpu.VMEM
@@ -460,12 +473,12 @@
             vmem((16, TILE), F32),
             vmem((NBIN * NCH, NCH), F32),
             vmem((8, NBIN * TILE), F32),
-            vmem((plane, 2, TILE), F32),
-            vmem((plane, 2, TILE), F32),
-            vmem((2, TILE), F32),
-            vmem((depth, 2, TILE), F32),
-            vmem((2, TILE), F32),
-            vmem((plane, 2, TILE), F32),
+            vmem((pieces, lines, TILE), F32),
+            vmem((plane, lines, TILE), F32),
+            vmem((lines, TILE), F32),
+            vmem((depth, lines, TILE), F32),
+            vmem((lines, TILE), F32),
+            vmem((pieces, lines, TILE), F32),
             vmem((NCH // 2, TILE), F32),
             dma((6,)),
             dma((chans,)),

time: 42.1 us -> 41.3 us (0.981)
  Pallas kernels: 40 us -> 39.2 us
    pallas_call x1, Pallas kernels: 40 us -> 39.2 us  [per_device(): pl.pallas_call(functools.partial(body, chans, patches), out_shape=(pltpu....]
where the time goes in v4:
time: 41.3 us; the launch traced here: 41.1 us
  Pallas kernels  39.2 us (95%)
  local copies, waits for them, and re-layouts  1.32 us (3%)
  between operations  0.64 us (2%)
    pallas_call x1, Pallas kernels, per_device(): pl.pallas_call(functools.partial(body, chans, patches), out_shape=(pltpu....  39.2 us
    unnamed x2, local copies, waits for them, and re-layouts  1.32 us

profile of v4, /device:TPU:1, one launch (start us, length us, event | category | flops | bytes accessed | tf_op | source)
XLA Modules:
  0.0 41.1 jit_solution(2247374478861143763)
XLA Ops:
  0.6 39.2 %sky_pairs.1 = (f32[8,64,64]{2,1,0:T(8,128)S(1)}, f32[64,64]{1,0:T(8,128)S(1)}) custom-call(f32[4,12288]{1,0:T(4,128)} %sky.1, f32[8,64]{1,0:T(8,128)} %bitcast.6, f32[96,1,128]{2,1,0:T(1,128)} %bitcast.5, s32[3,2,9]{2,1,0:T(2,128)} %nbr.1, s32[2,3]{1,0:T(2,128)} %bitcast.7, s32[9,128,128]{2,1,0:T(8,128)} %bins.1), custom_call_target="tpu_custom_call" | custom-call | tf_op jit(solution)/shard_map/sky_pairs/pallas_call | solution.py:447
  39.8 0.7 %copy.10 = f32[1,1,8,64,64]{4,3,2,1,0:T(8,128)} copy(f32[1,1,8,64,64]{4,3,2,1,0:T(8,128)S(1)} %bitcast.4) | data formatting | bytes 262144
  40.5 0.6 %copy.11 = f32[64,64]{1,0:T(8,128)} copy(f32[64,64]{1,0:T(8,128)S(1)} %get-tuple-element.7) | data formatting | bytes 32768

commit v5 on v4

--- a/solution.py
+++ b/solution.py
@@ -272,13 +272,21 @@
     ).astype(BF16)
     part = lax.dot_general(masked, weighted, NT, preferred_element_type=F32)
     half = NCH // 2
-    pieces = side * CORES
-    lines = half // pieces
-    packed = jnp.concatenate([part[:half], part[half:]], axis=1)
+    quarter = half // 2
+    pieces = 2 * CORES
+    lines = quarter // pieces
+    below = lax.broadcasted_iota(jnp.int32, (half, half), 0)
+    beside = lax.broadcasted_iota(jnp.int32, (half, half), 1)
+    first, cross, second = part[:half, :half], part[:half, half:], part[half:, half:]
+    corner = jnp.where(beside <= below, first, second)
+    folded = jnp.concatenate([cross, corner], axis=1)
+    packed = jnp.concatenate([folded[:quarter], folded[quarter:]], axis=1)
+    second_diagonal = jnp.sum(jnp.where(beside == below, second, 0.0), axis=0, keepdims=True)
     total = jnp.sum(seen[...], axis=0) * TILE
+    extra = jnp.concatenate([second_diagonal, total[:, half:]], axis=1)
     for number in range(pieces):
         piece[number, 0:lines, :] = packed[number * lines : (number + 1) * lines, :]
-        piece[number, lines : lines + 1, :] = total
+        piece[number, lines : lines + 1, :] = extra
 
     def seat_of(chan_list, n):
         i, c = seats[n]
@@ -286,9 +294,9 @@
 
     def piece_of(chan_list, n):
         i, c = seats[n]
-        return chan_list[i] % side * CORES + cores[c]
-
-    own_piece = chan_x * CORES + core
+        return chan_list[i] % 2 * CORES + cores[c]
+
+    own_piece = chan_x % 2 * CORES + core
 
     def plane_start(n, source, target, send, recv_sem):
         i, c = seats[n]
@@ -400,35 +408,62 @@
     whole_out[...] = z_sum
     whole_in[own_piece] = z_sum
 
-    row_seats = [n for n, (i, c) in enumerate(seats) if shifts[i][0] == 0]
-    whole_copies = [
-        plane_start(n, whole_out, whole_in.at[own_piece], whole_send, whole_recv)
-        for n in row_seats
-    ]
+    mate = chan + 1 - 2 * (chan_x % 2)
+    mates = [(mate, 0), (mate, 1), (chan, 1)]
+
+    def whole_copy(n, source, slot):
+        other, c = mates[n]
+        return remote(
+            source, slot, whole_send.at[n], whole_recv.at[n], other, z * CORES + cores[c]
+        )
+
+    whole_copies = [whole_copy(n, whole_out, whole_in.at[own_piece]) for n in range(len(mates))]
+    for copy in whole_copies:
+        copy.start()
     scales = []
     for level in range(NBIN):
         chunk = w_acc[:, level * TILE : (level + 1) * TILE]
         scales.append(
             jnp.maximum(jnp.sum(jnp.sum(chunk, axis=0, keepdims=True), axis=1, keepdims=True), 1.0)
         )
-    for n, copy in zip(row_seats, whole_copies):
-        plane_wait(n, copy, whole_in, piece_of, whole_send, whole_recv)
+        taper = 0.75 + 0.25 * math.cos(math.pi * level / NBIN)
+        acc[level * NCH : (level + 1) * NCH, :] = (
+            taper * acc[level * NCH : (level + 1) * NCH, :] / scales[level]
+        )
+    for n, copy in enumerate(whole_copies):
+        other, c = mates[n]
+        slot = whole_in.at[other % 2 * CORES + cores[c]]
+        copy.wait_send()
+        whole_copy(n, slot, slot).wait_recv()
 
     for number in range(pieces):
         packed_ref[number * lines : (number + 1) * lines, :] = (
-            whole_in[number, 0:lines, :] / whole_in[number, lines : lines + 1, :]
+            whole_in[number, 0:lines, :] / whole_in[number, lines : lines + 1, TILE - 1 :]
         )
     merged = packed_ref[...]
-    covariance = jnp.concatenate([merged[:, :NCH], merged[:, NCH:]], axis=0)
+    unfolded = jnp.concatenate([merged[:, :NCH], merged[:, NCH:]], axis=0)
+    cross, corner = unfolded[:, :half], unfolded[:, half:]
+    turned = corner.T
+    second_diagonal = (
+        whole_in[0, lines : lines + 1, :half] / whole_in[0, lines : lines + 1, TILE - 1 :]
+    )
+    first = jnp.where(beside <= below, corner, turned)
+    second = jnp.where(beside > below, corner, turned)
+    second = jnp.where(beside == below, second_diagonal, second)
+    covariance = jnp.concatenate(
+        [
+            jnp.concatenate([first, cross], axis=1),
+            jnp.concatenate([cross.T, second], axis=1),
+        ],
+        axis=0,
+    )
     cov_out[...] = covariance
     only = covariance * identity()
     down = jnp.sqrt(jnp.sum(only, axis=1, keepdims=True) + 1e-06)
     across = jnp.sqrt(jnp.sum(only, axis=0, keepdims=True) + 1e-06)
-    norm = down * across
+    inverse = 1.0 / (down * across)
     for level in range(NBIN):
-        taper = 0.75 + 0.25 * math.cos(math.pi * level / NBIN)
-        rows = acc[level * NCH : (level + 1) * NCH, :]
-        corr[level] = taper * rows / (scales[level] * norm)
+        corr[level] = acc[level * NCH : (level + 1) * NCH, :] * inverse
 
 
 def per_device(sky_maps, mode_vectors, pixel_weight, neighbours, tile_counts, pair_bins):
@@ -437,8 +472,8 @@
     plane = chans * CORES
     depth = patches // CORES
     rows = chans * TILES
-    pieces = math.isqrt(chans) * CORES
-    lines = NCH // 2 // pieces + 1
+    pieces = 2 * CORES
+    lines = NCH // 4 // pieces + 1
     weight = pixel_weight.reshape(rows, 1, TILE)
     dma = pltpu.SemaphoreType.DMA
     vmem = pltpu.VMEM
@@ -479,7 +514,7 @@
             vmem((depth, lines, TILE), F32),
             vmem((lines, TILE), F32),
             vmem((pieces, lines, TILE), F32),
-            vmem((NCH // 2, TILE), F32),
+            vmem((NCH // 4, TILE), F32),
             dma((6,)),
             dma((chans,)),
             dma((chans,)),
@@ -491,8 +526,8 @@
             dma((plane,)),
             dma((depth,)),
             dma((depth,)),
-            dma((plane,)),
-            dma((plane,)),
+            dma((3,)),
+            dma((3,)),
             pltpu.SemaphoreType.REGULAR((max(1, (depth // 2).bit_length() - 1),)),
         ],
         compiler_params=pltpu.CompilerParams(collective_id=0, has_side_effects=True),

time: 41.3 us -> 40.3 us (0.976)
  Pallas kernels: 39.2 us -> 38.2 us
    pallas_call x1, Pallas kernels: 39.2 us -> 38.2 us  [per_device(): pl.pallas_call(functools.partial(body, chans, patches), out_shape=(pltpu....]
where the time goes in v5:
time: 40.3 us; the launch traced here: 40.2 us
  Pallas kernels  38.2 us (95%)
  local copies, waits for them, and re-layouts  1.32 us (3%)
  between operations  0.64 us (2%)
    pallas_call x1, Pallas kernels, per_device(): pl.pallas_call(functools.partial(body, chans, patches), out_shape=(pltpu....  38.2 us
    unnamed x2, local copies, waits for them, and re-layouts  1.32 us

profile of v5, /device:TPU:1, one launch (start us, length us, event | category | flops | bytes accessed | tf_op | source)
XLA Modules:
  0.0 40.2 jit_solution(11924594834074926041)
XLA Ops:
  0.6 38.2 %sky_pairs.1 = (f32[8,64,64]{2,1,0:T(8,128)S(1)}, f32[64,64]{1,0:T(8,128)S(1)}) custom-call(f32[4,12288]{1,0:T(4,128)} %sky.1, f32[8,64]{1,0:T(8,128)} %bitcast.6, f32[96,1,128]{2,1,0:T(1,128)} %bitcast.5, s32[3,2,9]{2,1,0:T(2,128)} %nbr.1, s32[2,3]{1,0:T(2,128)} %bitcast.7, s32[9,128,128]{2,1,0:T(8,128)} %bins.1), custom_call_target="tpu_custom_call" | custom-call | tf_op jit(solution)/shard_map/sky_pairs/pallas_call | solution.py:482
  38.9 0.7 %copy.10 = f32[1,1,8,64,64]{4,3,2,1,0:T(8,128)} copy(f32[1,1,8,64,64]{4,3,2,1,0:T(8,128)S(1)} %bitcast.4) | data formatting | bytes 262144
  39.6 0.6 %copy.11 = f32[64,64]{1,0:T(8,128)} copy(f32[64,64]{1,0:T(8,128)S(1)} %get-tuple-element.7) | data formatting | bytes 32768

commit v6 on v5

--- a/solution.py
+++ b/solution.py
@@ -464,6 +464,17 @@
     inverse = 1.0 / (down * across)
     for level in range(NBIN):
         corr[level] = acc[level * NCH : (level + 1) * NCH, :] * inverse
+
+
+def deliver(corr_in, cov_in, corr_out, cov_out, sems):
+    copies = [
+        pltpu.make_async_copy(corr_in, corr_out, sems.at[0]),
+        pltpu.make_async_copy(cov_in, cov_out, sems.at[1]),
+    ]
+    for copy in copies:
+        copy.start()
+    for copy in copies:
+        copy.wait()
 
 
 def per_device(sky_maps, mode_vectors, pixel_weight, neighbours, tile_counts, pair_bins):
@@ -533,6 +544,20 @@
         compiler_params=pltpu.CompilerParams(collective_id=0, has_side_effects=True),
         name="sky_pairs",
     )(sky_maps, mode_vectors.T, weight, neighbours, tile_counts.T, pair_bins)
+    correlation, covariance = pl.pallas_call(
+        deliver,
+        out_shape=(
+            jax.ShapeDtypeStruct((NBIN, NCH, NCH), F32),
+            jax.ShapeDtypeStruct((NCH, NCH), F32),
+        ),
+        in_specs=[in_vmem, in_vmem],
+        out_specs=(anywhere, anywhere),
+        scratch_shapes=[dma((2,))],
+        name="deliver",
+    )(
+        pltpu.with_memory_space_constraint(correlation, pltpu.VMEM),
+        pltpu.with_memory_space_constraint(covariance, pltpu.VMEM),
+    )
     return (correlation[None, None], covariance)
 
 

time: 40.3 us -> 39.7 us (0.985)
  local copies, waits for them, and re-layouts: 1.32 us -> 0 us
  Pallas kernels: 38.2 us -> 39 us
    unnamed x2 -> x0, local copies, waits for them, and re-layouts: 1.32 us -> none
    pallas_call x0 -> x1, Pallas kernels: none -> 0.72 us  [per_device(): pl.pallas_call(deliver, out_shape=(jax.ShapeDtypeStruct((NBIN, NCH, NCH),...]
where the time goes in v6:
time: 39.7 us; the launch traced here: 39.6 us
  Pallas kernels  39 us (98%)
  between operations  0.64 us (2%)
    pallas_call x1, Pallas kernels, per_device(): pl.pallas_call(functools.partial(body, chans, patches), out_shape=(pltpu....  38.2 us

profile of v6, /device:TPU:1, one launch (start us, length us, event | category | flops | bytes accessed | tf_op | source)
XLA Modules:
  0.0 39.6 jit_solution(12051080802908433088)
XLA Ops:
  0.6 38.2 %sky_pairs.1 = (f32[8,64,64]{2,1,0:T(8,128)S(1)}, f32[64,64]{1,0:T(8,128)S(1)}) custom-call(f32[4,12288]{1,0:T(4,128)} %sky.1, f32[8,64]{1,0:T(8,128)} %bitcast.5, f32[96,1,128]{2,1,0:T(1,128)} %bitcast.4, s32[3,2,9]{2,1,0:T(2,128)} %nbr.1, s32[2,3]{1,0:T(2,128)} %bitcast.6, s32[9,128,128]{2,1,0:T(8,128)} %bins.1), custom_call_target="tpu_custom_call" | custom-call | tf_op jit(solution)/shard_map/sky_pairs/pallas_call | solution.py:493
  38.9 0.7 %deliver.1 = (f32[8,64,64]{2,1,0:T(8,128)}, f32[64,64]{1,0:T(8,128)}) custom-call(f32[8,64,64]{2,1,0:T(8,128)S(1)} %get-tuple-element.6.corr_in, f32[64,64]{1,0:T(8,128)S(1)} %get-tuple-element.7.cov_in), custom_call_target="tpu_custom_call" | custom-call | tf_op jit(solution)/shard_map/deliver/pallas_call | solution.py:547

commit v7 on v6

--- a/solution.py
+++ b/solution.py
@@ -247,7 +247,6 @@
     w_acc[...] = jnp.zeros_like(w_acc)
 
     for i in range(chans - 1):
-        sky_copy(i).wait_send()
         remote(
             recv.at[behind[i]],
             recv.at[behind[i]],
@@ -306,10 +305,9 @@
         copy.start()
         return copy
 
-    def plane_wait(n, sent, target, slot_of, send, recv_sem):
+    def plane_wait(n, target, slot_of, send, recv_sem):
         i, c = seats[n]
         slot = target.at[slot_of(behind, n)]
-        sent.wait_send()
         remote(
             slot, slot, send.at[n], recv_sem.at[n], behind[i], z * CORES + cores[c]
         ).wait_recv()
@@ -359,8 +357,10 @@
                     ] = cut[t * NCH : (t + 1) * NCH, :]
                 w_binned[code, :, level * TILE : (level + 1) * TILE] = cut[TILES * NCH :, :]
 
+    for i in range(chans - 1):
+        sky_copy(i).wait_send()
     for n in range(len(seats)):
-        plane_wait(n, plane_copies[n], plane_in, seat_of, plane_send, plane_recv)
+        plane_wait(n, plane_in, seat_of, plane_send, plane_recv)
 
     plane_sum = jnp.sum(plane_in[...], axis=0)
     z_out[...] = plane_sum
@@ -377,6 +377,8 @@
     for copy in z_copies:
         copy.start()
 
+    for copy in plane_copies:
+        copy.wait_send()
     for copy in side_copies:
         copy.wait()
 
@@ -397,9 +399,8 @@
             [w_tiles] * NBIN, axis=1
         )
 
-    for d, copy in zip(steps, z_copies):
+    for d in steps:
         other = (z + depth - d) % depth
-        copy.wait_send()
         remote(
             z_in.at[other], z_in.at[other], z_send.at[d], z_recv.at[d], *z_device(other)
         ).wait_recv()
@@ -430,6 +431,8 @@
         acc[level * NCH : (level + 1) * NCH, :] = (
             taper * acc[level * NCH : (level + 1) * NCH, :] / scales[level]
         )
+    for copy in z_copies:
+        copy.wait_send()
     for n, copy in enumerate(whole_copies):
         other, c = mates[n]
         slot = whole_in.at[other % 2 * CORES + cores[c]]

time: 39.7 us -> 39.7 us (level)
  no operation moved by 1% of the time
where the time goes in v7:
time: 39.7 us; the launch traced here: 39.5 us
  Pallas kernels  38.9 us (98%)
  between operations  0.64 us (2%)
    pallas_call x1, Pallas kernels, per_device(): pl.pallas_call(functools.partial(body, chans, patches), out_shape=(pltpu....  38.2 us

profile of v7, /device:TPU:1, one launch (start us, length us, event | category | flops | bytes accessed | tf_op | source)
XLA Modules:
  0.0 39.5 jit_solution(12954874438352904419)
XLA Ops:
  0.6 38.2 %sky_pairs.1 = (f32[8,64,64]{2,1,0:T(8,128)S(1)}, f32[64,64]{1,0:T(8,128)S(1)}) custom-call(f32[4,12288]{1,0:T(4,128)} %sky.1, f32[8,64]{1,0:T(8,128)} %bitcast.5, f32[96,1,128]{2,1,0:T(1,128)} %bitcast.4, s32[3,2,9]{2,1,0:T(2,128)} %nbr.1, s32[2,3]{1,0:T(2,128)} %bitcast.6, s32[9,128,128]{2,1,0:T(8,128)} %bins.1), custom_call_target="tpu_custom_call" | custom-call | tf_op jit(solution)/shard_map/sky_pairs/pallas_call | solution.py:496
  38.8 0.7 %deliver.1 = (f32[8,64,64]{2,1,0:T(8,128)}, f32[64,64]{1,0:T(8,128)}) custom-call(f32[8,64,64]{2,1,0:T(8,128)S(1)} %get-tuple-element.6.corr_in, f32[64,64]{1,0:T(8,128)S(1)} %get-tuple-element.7.cov_in), custom_call_target="tpu_custom_call" | custom-call | tf_op jit(solution)/shard_map/deliver/pallas_call | solution.py:550
